TPU v7x, 32 devices: a whole 2x2x4 slice. The times are simulated.
32 devices in a mesh: rx: 8 (over z, core), ry: 4 (over y, x).
Axes of the slice: x: 2, y: 2, z: 4, core: 2. Of those that a mesh axis runs over, the one named last changes fastest.
Arguments:
- record: bfloat16 [256, 256, 2048], P('rx', 'ry'), may hold values from -6 to 6
- sampled: int32 [256, 256], P('rx', 'ry'), may hold values 0 or 1
- levels: int32 [2], replicated, may hold values from 40 to 160
Outputs:
- restored: bfloat16 [256, 256, 2048], P('rx', 'ry')
All inputs are finite; a program needn't handle non-finite values. No bound on the sum of `sampled` on one device may be relied on, other than what follows from the above.
Results may differ from a plain program's by a relative error of at most 0.0027.
Values may be sent and summed in bfloat16 or wider, within the bound.
A program may use at most 128 MiB of HBM per device.

v0:
```python
import math

import jax
import jax.numpy as jnp
from jax import lax
from jax.sharding import PartitionSpec as P

H = 16
NF = 128
FLO = 8
ITERS = 2


def angles(row_ids, column_ids, period):
    products = row_ids[:, None] * column_ids[None, :] % period
    return products.astype(jnp.float32) * (2.0 * math.pi / period)


def taper(interior, margin):
    offsets = jnp.arange(interior + 2 * margin).astype(jnp.float32)
    rising = jnp.sin(0.5 * math.pi * (offsets + 0.5) / (2 * margin))
    falling = jnp.cos(0.5 * math.pi * (offsets - interior + 0.5) / (2 * margin))
    return jnp.where(
        offsets < 2 * margin,
        rising,
        jnp.where(offsets >= interior, falling, jnp.ones_like(offsets)),
    )


def time_forward(samples, bin_ids):
    phases = angles(jnp.arange(samples), bin_ids, samples)
    return jnp.stack([jnp.cos(phases), -jnp.sin(phases)], axis=1).astype(jnp.bfloat16)


def time_inverse(samples, bin_ids):
    phases = angles(bin_ids, jnp.arange(samples), samples)
    factor = 2.0 / samples
    return jnp.stack([jnp.cos(phases) * factor, -jnp.sin(phases) * factor], axis=1).astype(
        jnp.bfloat16
    )


def tile_forward(interior, margin):
    length = interior + 2 * margin
    offsets = jnp.arange(length)
    phases = angles(offsets, offsets, length)
    weights = taper(interior, margin)[None, :]
    cosine = (weights * jnp.cos(phases)).astype(jnp.bfloat16)
    sine_table = (weights * jnp.sin(phases)).astype(jnp.bfloat16)
    real_rows = jnp.stack([cosine, sine_table], axis=1)
    imag_rows = jnp.stack([-sine_table, cosine], axis=1)
    return jnp.stack([real_rows, imag_rows], axis=0)


def tile_inverse(interior, margin):
    length = interior + 2 * margin
    offsets = jnp.arange(length)
    phases = angles(offsets, offsets, length)
    weights = (taper(interior, margin) * (1.0 / length))[:, None]
    cosine = (weights * jnp.cos(phases)).astype(jnp.bfloat16)
    sine_table = (weights * jnp.sin(phases)).astype(jnp.bfloat16)
    real_rows = jnp.stack([cosine, -sine_table], axis=1)
    imag_rows = jnp.stack([sine_table, cosine], axis=1)
    return jnp.stack([real_rows, imag_rows], axis=0)


def plane_forward(positions, halves, length):
    columns = jnp.arange(2 * length)
    phases = angles(positions, columns % length, length)
    matched = halves[:, None] == (columns // length)[None, :]
    signed = jnp.where(halves[:, None] == 0, -1.0, 1.0) * jnp.sin(phases)
    return jnp.where(matched, jnp.cos(phases), signed).astype(jnp.bfloat16)


def plane_inverse(positions, halves, length):
    rows_all = jnp.arange(2 * length)
    phases = angles(rows_all % length, positions, length)
    factor = 1.0 / length
    matched = (rows_all // length)[:, None] == halves[None, :]
    signed = jnp.where((rows_all // length)[:, None] == 0, 1.0, -1.0) * (jnp.sin(phases) * factor)
    return jnp.where(matched, jnp.cos(phases) * factor, signed).astype(jnp.bfloat16)


def intersection_add(pieces, interior, margin):
    middle = pieces[:, :, margin : margin + interior].astype(jnp.float32)
    from_left = jnp.roll(pieces[:, :, interior + margin :], 1, axis=1).astype(jnp.float32)
    from_right = jnp.roll(pieces[:, :, :margin], -1, axis=1).astype(jnp.float32)
    filler = jnp.zeros(middle.shape[:2] + (interior - 2 * margin,) + middle.shape[3:], jnp.float32)
    extra = jnp.concatenate([from_left, filler, from_right], axis=2)
    return (middle + extra).astype(jnp.bfloat16)


def local_windows(columns, interior, margin):
    share, extent, width_all = columns.shape
    blocks = columns.reshape(share, extent // interior, interior, width_all)
    leading = jnp.roll(blocks, 1, axis=1)[:, :, interior - margin :]
    trailing = jnp.roll(blocks, -1, axis=1)[:, :, :margin]
    return jnp.concatenate([leading, blocks, trailing], axis=2)


def analyse(windows, forward_tile, forward_plane, across):
    share, tiles_count, length, width_all = windows.shape
    parted = windows.reshape(share, tiles_count, length, across, 2, width_all // (2 * across))
    turned = jnp.einsum(
        "qkps,fjsdpc->fjkdqc", forward_tile, parted, preferred_element_type=jnp.float32
    )
    turned = turned.astype(jnp.bfloat16).reshape(share * tiles_count * length, width_all)
    return jnp.dot(turned, forward_plane, preferred_element_type=jnp.float32)


def synthesise(shrunk, inverse_plane, inverse_tile, shape_all, across):
    share, tiles_count, length, width_all = shape_all
    planes = jnp.dot(shrunk, inverse_plane, preferred_element_type=jnp.float32).astype(jnp.bfloat16)
    planes = planes.reshape(share, tiles_count, length, across, 2, width_all // (2 * across))
    pieces = jnp.einsum(
        "qspk,fjkdpc->fjsdqc", inverse_tile, planes, preferred_element_type=jnp.float32
    )
    return pieces.astype(jnp.bfloat16).reshape(share, tiles_count, length, width_all)


def body(record, sampled, levels):
    rows_x, rows_y, samples = record.shape
    across = lax.axis_size("rx")
    down = lax.axis_size("ry")
    total_x = rows_x * across
    bin_ids = FLO + jnp.arange(NF)
    forward_time = time_forward(samples, bin_ids)
    forward_tile = tile_forward(rows_y, H)
    inverse_tile = tile_inverse(rows_y, H)
    flat_ids = jnp.arange(2 * total_x)
    positions = flat_ids // (2 * rows_x) * rows_x + flat_ids % rows_x
    halves = flat_ids // rows_x % 2
    forward_plane = plane_forward(positions, halves, total_x)
    inverse_plane = plane_inverse(positions, halves, total_x)
    inverse_time = time_inverse(samples, bin_ids)
    kept = sampled.astype(jnp.float32)[:, :, None]
    current = jnp.where(sampled[:, :, None] > 0, record, jnp.zeros((), jnp.bfloat16))
    for iteration in range(ITERS):
        spectra = jnp.einsum(
            "xyt,tpf->fypx", current, forward_time, preferred_element_type=jnp.float32
        )
        spectra = spectra.astype(jnp.bfloat16).reshape(NF, rows_y, 2 * rows_x)
        gathered = lax.all_to_all(spectra, ("rx", "ry"), split_axis=0, concat_axis=1, tiled=True)
        share = gathered.shape[0]
        columns = gathered.reshape(share, across, down * rows_y, 2 * rows_x)
        columns = jnp.transpose(columns, (0, 2, 1, 3)).reshape(share, down * rows_y, 2 * total_x)
        windows = local_windows(columns, rows_y, H)
        coeffs = analyse(windows, forward_tile, forward_plane, across)
        real_part = coeffs[:, :total_x]
        imag_part = coeffs[:, total_x:]
        magnitude = jnp.sqrt(real_part * real_part + imag_part * imag_part)
        largest = lax.pmax(jnp.max(magnitude), ("rx", "ry"))
        cutoff = levels[iteration].astype(jnp.float32) * 0.001 * (largest + 1e-06)
        shrink = jnp.maximum(magnitude - cutoff, 0.0) / jnp.maximum(magnitude, cutoff)
        shrunk = (coeffs * jnp.concatenate([shrink, shrink], axis=1)).astype(jnp.bfloat16)
        pieces = synthesise(shrunk, inverse_plane, inverse_tile, windows.shape, across)
        share = pieces.shape[0]
        merged = intersection_add(pieces, rows_y, H).reshape(
            share, down * rows_y, across, 2 * rows_x
        )
        merged = jnp.transpose(merged, (0, 2, 1, 3)).reshape(
            share, across * down * rows_y, 2 * rows_x
        )
        returned = lax.all_to_all(merged, ("rx", "ry"), split_axis=1, concat_axis=0, tiled=True)
        recon = jnp.einsum(
            "fypx,fpt->xyt",
            returned.reshape(NF, rows_y, 2, rows_x),
            inverse_time,
            preferred_element_type=jnp.float32,
        )
        current = (kept * record.astype(jnp.float32) + (1.0 - kept) * recon).astype(jnp.bfloat16)
    return current


def solution(mesh):
    return jax.shard_map(
        body,
        mesh=mesh,
        in_specs=(P("rx", "ry", None), P("rx", "ry"), P()),
        out_specs=P("rx", "ry", None),
        check_vma=False,
    )
```

profile of v0, /device:TPU:9, one launch (start us, length us, event | category | flops | bytes accessed | tf_op | source)
XLA Modules:
  0.0 399.5 jit_solution(7859233345429092915)
XLA Ops:
  0.7 4.4 %cosine_convert_fusion = (bf16[2048,1,128]{2,0,1:T(8,128)(2,1)S(1)}, bf16[2048,1,128]{2,0,1:T(8,128)(2,1)S(1)}) fusion(s32[128]{0:T(128)S(1)} %iota_add_fusion), kind=kLoop, calls=%fused_computation.92 | loop fusion | flops 4456448 | bytes 1049088 | tf_op jit(solution)/shard_map/convert
  5.2 6.1 %fusion.46 = bf16[2,128,32,64]{1,3,2,0:T(8,128)(2,1)S(1)} fusion(bf16[32,64,2048]{2,1,0:T(8,128)(2,1)} %param.3, pred[32,64]{1,0:T(8,128)(4,1)S(1)} %broadcast_compare_fusion, bf16[2048,1,128]{2,0,1:T(8,128)(2,1)S(1)} %get-tuple-element.34, bf16[2048,1,128]{2,0,1:T(8,128)(2,1)S(1)} %get-tuple-element.33), kind=kOutput, calls=%fused_computation.74 | convolution fusion | flops 2154299392 | bytes 10487808 | tf_op jit(solution)/shard_map/xyt,tpf->fypx/dot_general | solution.py:139
  11.3 3.5 copy.41
  14.9 2.2 reshape.700
  17.1 6.6 %all-to-all-start = ((bf16[32,2,8192]{2,1,0:T(2,128)(2,1)}), bf16[32,2,8192]{2,1,0:T(2,128)(2,1)S(1)}, u32[]{:S(2)}, u32[]{:S(2)}) async-start(bf16[32,2,8192]{2,1,0:T(2,128)(2,1)} %reshape.700), calls=%async_computation | async-start | bytes 2097152 | tf_op jit(solution)/shard_map/all_to_all | solution.py:143
  26.2 22.7 %all-to-all-done = bf16[32,2,8192]{2,1,0:T(2,128)(2,1)S(1)} async-done(((bf16[32,2,8192]{2,1,0:T(2,128)(2,1)}), bf16[32,2,8192]{2,1,0:T(2,128)(2,1)S(1)}, u32[]{:S(2)}, u32[]{:S(2)}) %all-to-all-start) | async-done | bytes 1048608 | tf_op jit(solution)/shard_map/all_to_all | solution.py:143
  48.9 1.3 reshape.701
  50.2 3.8 copy.42
  54.1 3.2 reshape.667
  57.3 1.8 reshape.698
  59.1 1.8 copy.43
  62.4 1.4 copy-done
  63.8 2.1 copy.47
  67.0 1.7 copy.44
  68.7 4.2 %fusion.33 = bf16[4,4,96,8,2,32]{2,5,4,3,1,0:T(8,128)(2,1)S(1)} fusion(bf16[4,4,16,8,2,32]{2,5,4,3,1,0:T(8,128)(2,1)S(1)} %bitcast.197, bf16[4,4,64,8,2,32]{2,5,4,3,1,0:T(8,128)(2,1)} %copy.47, bf16[4,4,16,8,2,32]{2,5,4,3,1,0:T(8,128)(2,1)} %bitcast.199, bf16[1,96,2,96]{3,1,2,0:T(8,128)(2,1)S(1)} %get-tuple-element.24, ...), kind=kOutput, calls=%fused_computation.51 | convolution fusion | flops 307642368 | bytes 3219456 | tf_op jit(solution)/shard_map/qkps,fjsdpc->fjkdqc/dot_general | solution.py:104
  73.0 1.6 copy.48
  74.6 3.7 reshape.668
  78.3 6.5 %fusion.68 = f32[1536,512]{0,1:T(8,128)S(1)} fusion(bf16[1536,512]{0,1:T(8,128)(2,1)} %reshape.668, f32[512]{0:T(512)S(1)} %compare_select_fusion, s32[512]{0:T(512)S(1)} %get-tuple-element.37, s32[512]{0:T(512)S(1)} %get-tuple-element.40, s32[512]{0:T(512)S(1)} %get-tuple-element.38, s32[512]{0:T(512)S(1)} %get-tuple-element.39), kind=kOutput, calls=%fused_computation.102 | convolution fusion | flops 810024960 | bytes 4728832 | tf_op jit(solution)/shard_map/dot_general | solution.py:108
  86.1 39.2 %pmax.14 = f32[]{:T(128)} all-reduce(f32[]{:T(128)} %fusion.69), channel_id=1, replica_groups=mesh['rx'=8,'ry'=4] {'rx','ry'}, use_global_device_ids=true, to_apply=%region_1.2 | all-reduce | flops 1 | bytes 8 | tf_op jit(solution)/shard_map/pmax | solution.py:152
  126.7 6.5 %convolution_convert_fusion.1 = bf16[1536,512]{1,0:T(8,128)(2,1)} fusion(f32[1536,512]{0,1:T(8,128)S(1)} %fusion.68, f32[1536,256]{0,1:T(8,128)S(1)} %maximum_divide_fusion.1, f32[512]{0:T(512)S(1)} %select_multiply_fusion, s32[512]{0:T(512)S(1)} %get-tuple-element.40, s32[512]{0:T(512)S(1)} %get-tuple-element.37, s32[512]{0:T(512)S(1)} %get-tuple-element.39, ...), kind=kOutput, calls=%fused_computation.26 | convolution fusion | flops 813432832 | bytes 6301696 | tf_op jit(solution)/shard_map/dot_general | solution.py:113
  133.2 2.6 copy.49
  135.8 4.3 %reshape.669 = bf16[4,4,96,8,2,32]{2,1,0,5,4,3:T(4,128)(2,1)S(1)} reshape(bf16[1536,512]{0,1:T(8,128)(2,1)} %copy.49) | data formatting | bytes 3145728 | tf_op jit(solution)/shard_map/reshape | solution.py:114
  142.0 2.3 fusion.126
  145.5 1.7 copy.106
  148.2 1.3 fusion.22
  149.6 2.8 reshape.671
  152.4 2.9 copy.96
  155.3 5.1 %reshape.702 = bf16[32,2,8192]{2,1,0:T(2,128)(2,1)} reshape(bf16[2048,4,64]{2,1,0:T(4,128)(2,1)} %bitcast.190) | data formatting | bytes 2097152
  160.4 5.6 %all-to-all-start.1 = ((bf16[32,2,8192]{2,1,0:T(2,128)(2,1)}), bf16[32,2,8192]{2,1,0:T(2,128)(2,1)S(1)}, u32[]{:S(2)}, u32[]{:S(2)}) async-start(bf16[32,2,8192]{2,1,0:T(2,128)(2,1)} %reshape.702), calls=%async_computation.1 | async-start | bytes 2097152 | tf_op jit(solution)/shard_map/all_to_all | solution.py:164
  166.0 5.7 %multiply_convert_fusion.1 = (bf16[128,1,2048]{2,0,1:T(8,128)(2,1)}, bf16[128,1,2048]{2,0,1:T(8,128)(2,1)}) fusion(s32[128]{0:T(128)S(1)} %iota_add_fusion), kind=kLoop, calls=%fused_computation.96 | loop fusion | flops 4980736 | bytes 1049088 | tf_op jit(solution)/shard_map/convert.2
  171.7 19.6 %all-to-all-done.1 = bf16[32,2,8192]{2,1,0:T(2,128)(2,1)S(1)} async-done(((bf16[32,2,8192]{2,1,0:T(2,128)(2,1)}), bf16[32,2,8192]{2,1,0:T(2,128)(2,1)S(1)}, u32[]{:S(2)}, u32[]{:S(2)}) %all-to-all-start.1) | async-done | bytes 1048608 | tf_op jit(solution)/shard_map/all_to_all | solution.py:164
  191.3 1.3 reshape.703
  192.6 2.4 copy.58
  195.0 11.3 %fusion.41 = bf16[2,128,32,64]{1,3,2,0:T(8,128)(2,1)S(1)} fusion(bf16[32,64,2048]{2,1,0:T(8,128)(2,1)} %param.3, f32[32,64]{1,0:T(8,128)S(1)} %broadcast_subtract_fusion, f32[32,64]{1,0:T(8,128)S(1)} %convert_element_type.274, bf16[128,64,2,32]{1,3,2,0:T(8,128)(2,1)} %bitcast.201, bf16[2048,1,128]{2,0,1:T(8,128)(2,1)} %copy-done.6, ...), kind=kOutput, calls=%fused_computation.73 | convolution fusion | flops 4320657408 | bytes 12599296 | tf_op jit(solution)/shard_map/xyt,tpf->fypx/dot_general | solution.py:139
  206.3 3.5 copy.60
  209.8 2.2 reshape.704
  212.1 5.1 %all-to-all-start.2 = ((bf16[32,2,8192]{2,1,0:T(2,128)(2,1)}), bf16[32,2,8192]{2,1,0:T(2,128)(2,1)S(1)}, u32[]{:S(2)}, u32[]{:S(2)}) async-start(bf16[32,2,8192]{2,1,0:T(2,128)(2,1)} %reshape.704), calls=%async_computation.2 | async-start | bytes 2097152 | tf_op jit(solution)/shard_map/all_to_all | solution.py:143
  217.7 24.6 %all-to-all-done.2 = bf16[32,2,8192]{2,1,0:T(2,128)(2,1)S(1)} async-done(((bf16[32,2,8192]{2,1,0:T(2,128)(2,1)}), bf16[32,2,8192]{2,1,0:T(2,128)(2,1)S(1)}, u32[]{:S(2)}, u32[]{:S(2)}) %all-to-all-start.2) | async-done | bytes 1048608 | tf_op jit(solution)/shard_map/all_to_all | solution.py:143
  242.3 1.3 reshape.705
  243.6 3.8 copy.61
  247.4 3.2 reshape.675
  250.7 1.8 reshape.699
  252.5 1.8 copy.62
  255.8 1.4 copy-done.1
  257.2 2.1 copy.66
  259.3 1.7 copy.65
  261.1 1.7 copy.63
  263.2 4.2 %fusion.34 = bf16[4,4,96,8,2,32]{2,5,4,3,1,0:T(8,128)(2,1)S(1)} fusion(bf16[4,4,16,8,2,32]{2,5,4,3,1,0:T(8,128)(2,1)S(1)} %bitcast.196, bf16[4,4,64,8,2,32]{2,5,4,3,1,0:T(8,128)(2,1)} %copy.66, bf16[4,4,16,8,2,32]{2,5,4,3,1,0:T(8,128)(2,1)} %bitcast.198, bf16[1,96,2,96]{3,1,2,0:T(8,128)(2,1)S(1)} %get-tuple-element.24, ...), kind=kOutput, calls=%fused_computation.52 | convolution fusion | flops 307642368 | bytes 3219456 | tf_op jit(solution)/shard_map/qkps,fjsdpc->fjkdqc/dot_general | solution.py:104
  267.4 1.6 copy.67
  269.1 3.4 reshape.676
  272.4 6.5 %fusion.67 = f32[1536,512]{0,1:T(8,128)S(1)} fusion(bf16[1536,512]{0,1:T(8,128)(2,1)} %reshape.676, f32[512]{0:T(512)S(1)} %compare_select_fusion, s32[512]{0:T(512)S(1)} %get-tuple-element.37, s32[512]{0:T(512)S(1)} %get-tuple-element.40, s32[512]{0:T(512)S(1)} %get-tuple-element.38, s32[512]{0:T(512)S(1)} %get-tuple-element.39), kind=kOutput, calls=%fused_computation.101 | convolution fusion | flops 810024960 | bytes 4728832 | tf_op jit(solution)/shard_map/dot_general | solution.py:108
  280.2 39.3 %pmax.15 = f32[]{:T(128)} all-reduce(f32[]{:T(128)} %fusion.70), channel_id=1, replica_groups=mesh['rx'=8,'ry'=4] {'rx','ry'}, use_global_device_ids=true, to_apply=%region_3.4 | all-reduce | flops 1 | bytes 8 | tf_op jit(solution)/shard_map/pmax | solution.py:152
  320.9 6.5 %convolution_convert_fusion = bf16[1536,512]{1,0:T(8,128)(2,1)} fusion(f32[1536,512]{0,1:T(8,128)S(1)} %fusion.67, f32[1536,256]{0,1:T(8,128)S(1)} %maximum_divide_fusion, f32[512]{0:T(512)S(1)} %select_multiply_fusion, s32[512]{0:T(512)S(1)} %get-tuple-element.40, s32[512]{0:T(512)S(1)} %get-tuple-element.37, s32[512]{0:T(512)S(1)} %get-tuple-element.39, ...), kind=kOutput, calls=%fused_computation.25 | convolution fusion | flops 813432832 | bytes 6301696 | tf_op jit(solution)/shard_map/dot_general | solution.py:113
  327.5 2.6 copy.68
  330.1 4.3 %reshape.677 = bf16[4,4,96,8,2,32]{2,1,0,5,4,3:T(4,128)(2,1)S(1)} reshape(bf16[1536,512]{0,1:T(8,128)(2,1)} %copy.68) | data formatting | bytes 3145728 | tf_op jit(solution)/shard_map/reshape | solution.py:114
  336.2 2.3 fusion.124
  339.8 1.7 copy.111
  342.5 1.3 fusion.27
  343.9 2.8 reshape.679
  346.7 2.9 copy.101
  349.6 4.4 %reshape.706 = bf16[32,2,8192]{2,1,0:T(2,128)(2,1)S(1)} reshape(bf16[2048,4,64]{2,1,0:T(4,128)(2,1)} %bitcast.194) | data formatting | bytes 2097152
  354.0 30.7 %all_to_all.60 = bf16[32,2,8192]{2,1,0:T(2,128)(2,1)S(1)} all-to-all(bf16[32,2,8192]{2,1,0:T(2,128)(2,1)S(1)} %reshape.706), channel_id=1, replica_groups=mesh['rx'=8,'ry'=4] {'rx','ry'}, dimensions={0} | all-to-all | bytes 2097152 | tf_op jit(solution)/shard_map/all_to_all | solution.py:164
  386.0 2.4 copy.77
  388.4 10.9 %fusion.1 = bf16[32,64,2048]{2,1,0:T(8,128)(2,1)} fusion(bf16[32,64,2048]{2,1,0:T(8,128)(2,1)} %param.3, f32[32,64]{1,0:T(8,128)S(1)} %broadcast_subtract_fusion, f32[32,64]{1,0:T(8,128)S(1)} %convert_element_type.274, bf16[128,64,2,32]{1,3,2,0:T(8,128)(2,1)} %bitcast.200, bf16[128,1,2048]{2,0,1:T(8,128)(2,1)S(1)} %copy-done.8, ...), kind=kOutput, calls=%fused_computation.2 | convolution fusion | flops 2170552320 | bytes 18890752 | tf_op jit(solution)/shard_map/fypx,fpt->xyt/dot_general | solution.py:165
  (72 shorter events, 20.3 us)
Async XLA Ops:
  5.2 6.2 %copy-start.5 = (bf16[2048,1,128]{2,0,1:T(8,128)(2,1)}, bf16[2048,1,128]{2,0,1:T(8,128)(2,1)S(1)}, u32[]{:S(2)}) copy-start(bf16[2048,1,128]{2,0,1:T(8,128)(2,1)S(1)} %get-tuple-element.33) | copy-start | bytes 1572868
  5.2 6.2 %copy-start.6 = (bf16[2048,1,128]{2,0,1:T(8,128)(2,1)}, bf16[2048,1,128]{2,0,1:T(8,128)(2,1)S(1)}, u32[]{:S(2)}) copy-start(bf16[2048,1,128]{2,0,1:T(8,128)(2,1)S(1)} %get-tuple-element.34) | copy-start | bytes 1572868
  14.9 8.9 %copy-start.10 = (s32[2]{0:T(128)S(1)}, s32[2]{0:T(128)}, u32[]{:S(2)}) copy-start(s32[2]{0:T(128)} %param.5) | copy-start | bytes 28
  17.1 31.8 %all-to-all-start = ((bf16[32,2,8192]{2,1,0:T(2,128)(2,1)}), bf16[32,2,8192]{2,1,0:T(2,128)(2,1)S(1)}, u32[]{:S(2)}, u32[]{:S(2)}) async-start(bf16[32,2,8192]{2,1,0:T(2,128)(2,1)} %reshape.700), calls=%async_computation | async-start | bytes 2097152 | tf_op jit(solution)/shard_map/all_to_all | solution.py:143
  62.2 1.6 copy-start
  145.5 1.9 copy-start.2
  155.3 10.7 %copy-start.9 = (s32[32,64]{1,0:T(8,128)S(1)}, s32[32,64]{1,0:T(8,128)}, u32[]{:S(2)}) copy-start(s32[32,64]{1,0:T(8,128)} %param.4) | copy-start | bytes 24580
  160.4 30.9 %all-to-all-start.1 = ((bf16[32,2,8192]{2,1,0:T(2,128)(2,1)}), bf16[32,2,8192]{2,1,0:T(2,128)(2,1)S(1)}, u32[]{:S(2)}, u32[]{:S(2)}) async-start(bf16[32,2,8192]{2,1,0:T(2,128)(2,1)} %reshape.702), calls=%async_computation.1 | async-start | bytes 2097152 | tf_op jit(solution)/shard_map/all_to_all | solution.py:164
  212.1 30.2 %all-to-all-start.2 = ((bf16[32,2,8192]{2,1,0:T(2,128)(2,1)}), bf16[32,2,8192]{2,1,0:T(2,128)(2,1)S(1)}, u32[]{:S(2)}, u32[]{:S(2)}) async-start(bf16[32,2,8192]{2,1,0:T(2,128)(2,1)} %reshape.704), calls=%async_computation.2 | async-start | bytes 2097152 | tf_op jit(solution)/shard_map/all_to_all | solution.py:143
  255.6 1.6 copy-start.1
  261.1 2.1 copy-start.4
  339.7 1.9 copy-start.3
  386.0 2.4 copy-start.7
  386.0 2.4 copy-start.8
where the time goes:
time: 407 us; the launch traced here: 400 us
  local copies, waits for them, and re-layouts  119 us (29%)
  blocking collectives  109 us (27%)
  waiting for transfers between devices  66.9 us (16%)
  matrix products  64.8 us (16%)
  other arithmetic  18.8 us (5%)
  starting transfers between devices  17.2 us (4%)
    pmax x2, blocking collectives, body(): largest = lax.pmax(jnp.max(magnitude), ('rx', 'ry'))  78.5 us
    all_to_all x2, waiting for transfers between devices, body(): lax.all_to_all(spectra, ('rx', 'ry'), split_axis=0, concat_axis=1, tiled=...  47.3 us
    all_to_all x1, blocking collectives, body(): lax.all_to_all(merged, ('rx', 'ry'), split_axis=1, concat_axis=0, tiled=T...  30.7 us
    unnamed x40, local copies, waits for them, and re-layouts  30.2 us
    all_to_all x1, waiting for transfers between devices, body(): lax.all_to_all(merged, ('rx', 'ry'), split_axis=1, concat_axis=0, tiled=T...  19.6 us
    dot_general x2, matrix products, body(): jnp.einsum('xyt,tpf->fypx', current, forward_time, preferred_element_type...  17.5 us
    dot_general x2, matrix products, synthesise(): jnp.dot(shrunk, inverse_plane, preferred_element_type=jnp.float32)  13.1 us
    dot_general x2, matrix products, analyse(): return jnp.dot(turned, forward_plane, preferred_element_type=jnp.float32)  13 us
  transfers between devices with their start and end apart: 3, of which 3 were waited for; matrix products, arithmetic and copies ran while one was open for 2% of the time, Pallas kernels for 0%

commit v1 on v0

v1 whole, which is shorter than its diff:
```python
import functools
import math

import jax
import jax.numpy as jnp
import numpy as np
from jax import lax
from jax.experimental import pallas as pl
from jax.experimental.pallas import tpu as pltpu
from jax.sharding import PartitionSpec as P

H = 16
NF = 128
FLO = 8
ITERS = 2
LANES = 128
MISSING = float(2.0**100)
FOUND = float(2.0**90)
MESH = pl.DeviceIdType.MESH
VM = pl.BlockSpec(memory_space=pltpu.VMEM)
SM = pl.BlockSpec(memory_space=pltpu.SMEM)
ANY = pl.BlockSpec(memory_space=pl.ANY)


def rounded(table):
    return np.asarray(table, np.float32).astype(jnp.bfloat16)


def angles(rows, columns, period):
    return (rows[:, None] * columns[None, :] % period) * (2.0 * math.pi / period)


def time_table(samples, devices):
    share = NF // devices
    phases = angles(FLO + np.arange(NF), np.arange(samples), samples)
    both = np.stack([np.cos(phases), -np.sin(phases)]).reshape(2, devices, share, samples)
    return rounded(both.transpose(1, 0, 2, 3).reshape(2 * NF, samples))


def plane_tables(positions):
    length = positions.shape[0]
    phases = angles(np.arange(length), positions, length)
    c, s = np.cos(phases), np.sin(phases)
    forward = np.block([[c, s], [-s, c]])
    c, s = c.T / length, s.T / length
    inverse = np.block([[c, -s], [s, c]])
    return rounded(forward), rounded(inverse)


def tile_tables(interior, extent):
    length = interior + 2 * H
    tiles = extent // interior
    offsets = np.arange(length)
    taper = np.where(
        offsets < 2 * H,
        np.sin(0.5 * math.pi * (offsets + 0.5) / (2 * H)),
        np.where(offsets >= interior, np.cos(0.5 * math.pi * (offsets - interior + 0.5) / (2 * H)), 1.0),
    )
    phases = angles(offsets, offsets, length)
    c, s = np.cos(phases), np.sin(phases)
    forward = np.zeros((2, extent, 2, tiles, length))
    inverse = np.zeros((2, tiles, length, 2, extent))
    ya, yb = taper[:, None] * c, taper[:, None] * s
    yc, yd = c * (taper / length)[None, :], s * (taper / length)[None, :]
    for j in range(tiles):
        at = (j * interior - H + offsets) % extent
        for o in range(length):
            forward[0, at[o], 0, j] += ya[o]
            forward[1, at[o], 0, j] += yb[o]
            forward[0, at[o], 1, j] -= yb[o]
            forward[1, at[o], 1, j] += ya[o]
            inverse[0, j, :, 0, at[o]] += yc[:, o]
            inverse[1, j, :, 0, at[o]] -= yd[:, o]
            inverse[0, j, :, 1, at[o]] += yd[:, o]
            inverse[1, j, :, 1, at[o]] += yc[:, o]
    wide = 2 * tiles * length
    return rounded(forward.reshape(2 * extent, wide)), rounded(inverse.reshape(wide, 2 * extent))


def meet_all(across, down):
    devices = across * down
    me = lax.axis_index("rx") * down + lax.axis_index("ry")
    barrier = pltpu.get_barrier_semaphore()

    def greet(k, carry):
        peer = lax.rem(me + k, devices)
        pl.semaphore_signal(
            barrier, inc=1, device_id=(peer // down, lax.rem(peer, down)), device_id_type=MESH
        )
        return carry

    lax.fori_loop(1, devices, greet, 0)
    pl.semaphore_wait(barrier, devices - 1)
    return me


def exchange_kernel(across, down, per_peer, src, dst, send_sem, recv_sem, own_sem):
    devices = across * down
    me = meet_all(across, down)

    def outgoing(k):
        peer = lax.rem(me + k, devices)
        return pltpu.make_async_remote_copy(
            src_ref=src.at[peer] if per_peer else src,
            dst_ref=dst.at[me],
            send_sem=send_sem.at[peer],
            recv_sem=recv_sem.at[me],
            device_id=(peer // down, lax.rem(peer, down)),
            device_id_type=MESH,
        )

    def incoming(k):
        peer = lax.rem(me + k, devices)
        return pltpu.make_async_remote_copy(
            src_ref=src.at[peer] if per_peer else src,
            dst_ref=dst.at[peer],
            send_sem=send_sem.at[peer],
            recv_sem=recv_sem.at[peer],
            device_id=(peer // down, lax.rem(peer, down)),
            device_id_type=MESH,
        )

    def start(k, carry):
        outgoing(k).start()
        return carry

    def finish(k, carry):
        incoming(k).wait()
        return carry

    own = pltpu.make_async_copy(src.at[me] if per_peer else src, dst.at[me], own_sem)
    own.start()
    lax.fori_loop(1, devices, start, 0)
    own.wait()
    lax.fori_loop(1, devices, finish, 0)


def exchange(across, down, blocks, collective_id):
    devices = across * down
    return pl.pallas_call(
        functools.partial(exchange_kernel, across, down, True),
        out_shape=jax.ShapeDtypeStruct(blocks.shape, blocks.dtype),
        in_specs=[VM],
        out_specs=VM,
        scratch_shapes=[
            pltpu.SemaphoreType.DMA((devices,)),
            pltpu.SemaphoreType.DMA((devices,)),
            pltpu.SemaphoreType.DMA,
        ],
        compiler_params=pltpu.CompilerParams(collective_id=collective_id, has_side_effects=True),
    )(blocks)


def share_max(across, down, peaks):
    devices = across * down
    return pl.pallas_call(
        functools.partial(exchange_kernel, across, down, False),
        out_shape=jax.ShapeDtypeStruct((devices,) + peaks.shape, peaks.dtype),
        in_specs=[VM],
        out_specs=VM,
        scratch_shapes=[
            pltpu.SemaphoreType.DMA((devices,)),
            pltpu.SemaphoreType.DMA((devices,)),
            pltpu.SemaphoreType.DMA,
        ],
        compiler_params=pltpu.CompilerParams(collective_id=2, has_side_effects=True),
    )(peaks)


def dot(a, b):
    return jnp.dot(a, b, preferred_element_type=jnp.float32)


def analyse(sizes, grid, plane, tile, coeffs, peaks):
    nx, ny, share, half = sizes
    best = jnp.zeros((8, LANES), jnp.float32)
    for f in range(share):
        turned = dot(plane[...], grid[:, f * ny : (f + 1) * ny]).astype(jnp.bfloat16)
        c = dot(jnp.concatenate([turned[:nx], turned[nx:]], axis=1), tile[...])
        coeffs[f] = c
        re, im = c[:, :half], c[:, half:]
        power = re * re + im * im
        best = jnp.maximum(best, jnp.max(power.reshape(-1, 8, half), axis=0)[:, :LANES])
        for part in range(1, half // LANES):
            best = jnp.maximum(
                best,
                jnp.max(power[:, part * LANES : (part + 1) * LANES].reshape(-1, 8, LANES), axis=0),
            )
    peaks[...] = best


def synthesise(sizes, level, tops, coeffs, plane, tile):
    nx, ny, share, half = sizes
    largest = jnp.sqrt(jnp.max(jnp.max(tops[...], axis=0), keepdims=True))
    cutoff = level.astype(jnp.float32) * 0.001 * (largest + 1e-06)
    for f in range(share):
        re, im = coeffs[f, :, :half], coeffs[f, :, half:]
        magnitude = jnp.sqrt(re * re + im * im)
        shrink = jnp.maximum(magnitude - cutoff, 0.0) / jnp.maximum(magnitude, cutoff)
        shrunk = jnp.concatenate(
            [(re * shrink).astype(jnp.bfloat16), (im * shrink).astype(jnp.bfloat16)], axis=1
        )
        lines = dot(shrunk, tile[...]).astype(jnp.bfloat16)
        yield f, dot(plane[...], jnp.concatenate([lines[:, :ny], lines[:, ny:]], axis=0))


def first_kernel(sizes, shape, received, plane, tile, marked, coeffs, peaks, grid, left, right):
    across, down, interior, groups = shape
    nx, ny, share, half = sizes
    rows = 2 * share
    lower = lax.broadcasted_iota(jnp.int32, (groups, LANES), 1) < interior

    def gather(rx, carry):
        for pair in range(down // 2):
            for at, ref in ((0, left), (1, right)):
                block = received[rx * down + 2 * pair + at].astype(jnp.float32)
                for g in range(groups):
                    ref[g * rows : (g + 1) * rows] = block[:, g * LANES : (g + 1) * LANES]
            for r in range(rows):
                p, f = r // share, r % share
                a = left[pl.ds(r, groups, stride=rows)]
                b = right[pl.ds(r, groups, stride=rows)]
                first = jnp.where(lower, a, pltpu.roll(b, interior, 1)).astype(jnp.bfloat16)
                second = jnp.where(lower, pltpu.roll(a, interior, 1), b).astype(jnp.bfloat16)
                lanes = slice(f * ny + pair * LANES, f * ny + (pair + 1) * LANES)
                for xa, value in ((0, first), (1, second)):
                    row = pl.multiple_of(p * nx + (xa * across + rx) * groups, groups)
                    marked[pl.ds(row, groups), lanes] = value
        return carry

    lax.fori_loop(0, across, gather, 0)
    seen = marked[...].astype(jnp.float32)
    grid[...] = jnp.where(seen > FOUND, 0.0, seen).astype(jnp.bfloat16)
    analyse(sizes, grid, plane, tile, coeffs, peaks)


def again_kernel(
    sizes, iteration, levels, tops, old, marked, inv_tile, inv_plane, plane, tile, coeffs, peaks, grid
):
    nx, ny, share, half = sizes
    for f, back in synthesise(sizes, levels[iteration], tops, old, inv_plane, inv_tile):
        lanes = slice(f * ny, (f + 1) * ny)
        seen = marked[:, lanes].astype(jnp.float32)
        grid[:, lanes] = jnp.where(seen > FOUND, back, seen).astype(jnp.bfloat16)
    analyse(sizes, grid, plane, tile, coeffs, peaks)


def last_kernel(
    sizes, shape, iteration, levels, tops, old, inv_tile, inv_plane, sent, grid, left, right
):
    across, down, interior, groups = shape
    nx, ny, share, half = sizes
    rows = 2 * share
    for f, back in synthesise(sizes, levels[iteration], tops, old, inv_plane, inv_tile):
        grid[:, f * ny : (f + 1) * ny] = back
    lower = lax.broadcasted_iota(jnp.int32, (groups, LANES), 1) < interior

    def spread(rx, carry):
        for pair in range(down // 2):
            for r in range(rows):
                p, f = r // share, r % share
                lanes = slice(f * ny + pair * LANES, f * ny + (pair + 1) * LANES)
                first, second = (
                    grid[pl.ds(pl.multiple_of(p * nx + (xa * across + rx) * groups, groups), groups), lanes]
                    for xa in range(2)
                )
                left[pl.ds(r, groups, stride=rows)] = jnp.where(lower, first, pltpu.roll(second, interior, 1))
                right[pl.ds(r, groups, stride=rows)] = jnp.where(lower, pltpu.roll(first, interior, 1), second)
            for at, ref in ((0, left), (1, right)):
                for g in range(groups):
                    sent[rx * down + 2 * pair + at, :, g * LANES : (g + 1) * LANES] = ref[
                        g * rows : (g + 1) * rows
                    ].astype(jnp.bfloat16)
        return carry

    lax.fori_loop(0, across, spread, 0)


def body(across, down, record, sampled, levels):
    rows_x, rows_y, samples = record.shape
    devices = across * down
    share = NF // devices
    rows = 2 * share
    nx, ny = rows_x * across, rows_y * down
    traces = rows_x * rows_y
    pack = LANES // rows_y
    groups = traces // LANES
    assert pack == 2 and down % 2 == 0
    half = ny // rows_y * (rows_y + 2 * H)
    sizes = (nx, ny, share, half)
    shape = (across, down, rows_y, groups)
    times = jnp.asarray(time_table(samples, devices))
    ids = np.arange(nx)
    xa, rx, g = ids // (across * groups), ids // groups % across, ids % groups
    plane, inv_plane = map(jnp.asarray, plane_tables(rx * rows_x + g * pack + xa))
    tile, inv_tile = map(jnp.asarray, tile_tables(rows_y, ny))
    flat = record.reshape(traces, samples)
    spectra = lax.dot_general(
        times, flat, (((1,), (1,)), ((), ())), preferred_element_type=jnp.float32
    )
    spectra = jnp.where(sampled.reshape(1, traces) > 0, spectra, MISSING).astype(jnp.bfloat16)
    received = exchange(across, down, spectra.reshape(devices, rows, traces), 0)
    coeffs_type = jax.ShapeDtypeStruct((share, nx, 2 * half), jnp.float32)
    peaks_type = jax.ShapeDtypeStruct((8, LANES), jnp.float32)
    grid_shape = (2 * nx, share * ny)
    folded = [pltpu.VMEM((groups * rows, LANES), jnp.float32)] * 2
    params = pltpu.CompilerParams(vmem_limit_bytes=48 * 1024 * 1024)
    marked, coeffs, peaks = pl.pallas_call(
        functools.partial(first_kernel, sizes, shape),
        out_shape=(jax.ShapeDtypeStruct(grid_shape, jnp.bfloat16), coeffs_type, peaks_type),
        in_specs=[VM] * 3,
        out_specs=(VM,) * 3,
        scratch_shapes=[pltpu.VMEM(grid_shape, jnp.bfloat16)] + folded,
        compiler_params=params,
    )(received, plane, tile)
    for iteration in range(ITERS - 1):
        tops = share_max(across, down, peaks)
        coeffs, peaks = pl.pallas_call(
            functools.partial(again_kernel, sizes, iteration),
            out_shape=(coeffs_type, peaks_type),
            in_specs=[SM] + [VM] * 7,
            out_specs=(VM,) * 2,
            scratch_shapes=[pltpu.VMEM(grid_shape, jnp.bfloat16)],
            compiler_params=params,
        )(levels, tops, coeffs, marked, inv_tile, inv_plane, plane, tile)
    tops = share_max(across, down, peaks)
    sent = pl.pallas_call(
        functools.partial(last_kernel, sizes, shape, ITERS - 1),
        out_shape=jax.ShapeDtypeStruct((devices, rows, traces), jnp.bfloat16),
        in_specs=[SM] + [VM] * 4,
        out_specs=VM,
        scratch_shapes=[pltpu.VMEM(grid_shape, jnp.float32)] + folded,
        compiler_params=params,
    )(levels, tops, coeffs, inv_tile, inv_plane)
    returned = exchange(across, down, sent, 1)
    recon = lax.dot_general(
        returned.reshape(2 * NF, traces), times, (((0,), (0,)), ((), ())),
        preferred_element_type=jnp.float32,
    ).reshape(rows_x, rows_y, samples) * (2.0 / samples)
    return jnp.where(sampled[:, :, None] > 0, record.astype(jnp.float32), recon).astype(jnp.bfloat16)


def solution(mesh):
    return jax.shard_map(
        functools.partial(body, mesh.shape["rx"], mesh.shape["ry"]),
        mesh=mesh,
        in_specs=(P("rx", "ry", None), P("rx", "ry"), P()),
        out_specs=P("rx", "ry", None),
        check_vma=False,
    )
```

time: 407 us -> 127 us (0.31); the launches traced: 400 us -> 125 us
  blocking collectives: 109 us -> 0 us
  local copies, waits for them, and re-layouts: 119 us -> 10.8 us
  Pallas kernels: 0 us -> 99.2 us
  waiting for transfers between devices: 66.9 us -> 0 us
  matrix products: 64.8 us -> 14.1 us
  other arithmetic: 18.8 us -> 0.72 us
  starting transfers between devices: 17.2 us -> 0 us
    pallas_call x0 -> x7, Pallas kernels: none -> 99.2 us  [the longest x2 60 us: exchange(): pl.pallas_call(functools.partial(exchange_kernel, across, down, True), ou...]
    pmax x2 -> x0, blocking collectives: 78.5 us -> none  [body(): largest = lax.pmax(jnp.max(magnitude), ('rx', 'ry'))]
    all_to_all x3 -> x0, waiting for transfers between devices: 66.9 us -> none  [the longest x2 47.3 us: body(): lax.all_to_all(spectra, ('rx', 'ry'), split_axis=0, concat_axis=1, tiled=...]
    dot_general x11 -> x2, matrix products: 64.8 us -> 14.1 us  [the longest x1 7.19 us: body(): lax.dot_general(times, flat, (((1,), (1,)), ((), ())), preferred_element_...]
    reshape x12 -> x0, local copies, waits for them, and re-layouts: 40.7 us -> none  [the longest x2 8.67 us: synthesise(): planes.reshape(share, tiles_count, length, across, 2, width_all // (2 * a...]
    all_to_all x1 -> x0, blocking collectives: 30.7 us -> none  [body(): lax.all_to_all(merged, ('rx', 'ry'), split_axis=1, concat_axis=0, tiled=T...]
    unnamed x40 -> x30, local copies, waits for them, and re-layouts: 30.2 us -> 9.28 us
    all_to_all x3 -> x0, starting transfers between devices: 17.2 us -> none  [the longest x2 11.7 us: body(): lax.all_to_all(spectra, ('rx', 'ry'), split_axis=0, concat_axis=1, tiled=...]
  transfers between devices with their start and end apart: 3 -> 0, of which waited for: 3 -> 0; matrix products, arithmetic and copies ran while one was open for 2% -> 0% of each run, Pallas kernels for 0% -> 0%
where the time goes in v1:
time: 127 us; the launch traced here: 125 us
  Pallas kernels  99.2 us (78%)
  matrix products  14.1 us (11%)
  local copies, waits for them, and re-layouts  10.8 us (9%)
    pallas_call x2, Pallas kernels, exchange(): pl.pallas_call(functools.partial(exchange_kernel, across, down, True), ou...  60 us
    pallas_call x2, Pallas kernels, share_max(): pl.pallas_call(functools.partial(exchange_kernel, across, down, False), o...  22.3 us
    unnamed x30, local copies, waits for them, and re-layouts  9.28 us
    pallas_call x1, Pallas kernels, body(): pl.pallas_call(functools.partial(again_kernel, sizes, iteration), out_sha...  7.79 us
    dot_general x1, matrix products, body(): lax.dot_general(times, flat, (((1,), (1,)), ((), ())), preferred_element_...  7.19 us
    dot_general x1, matrix products, body(): lax.dot_general(returned.reshape(2 * NF, traces), times, (((0,), (0,)), (...  6.94 us
    pallas_call x1, Pallas kernels, body(): pl.pallas_call(functools.partial(first_kernel, sizes, shape), out_shape=(...  5.05 us
    pallas_call x1, Pallas kernels, body(): pl.pallas_call(functools.partial(last_kernel, sizes, shape, ITERS - 1), o...  4.02 us

profile of v1, /device:TPU:9, one launch (start us, length us, event | category | flops | bytes accessed | tf_op | source)
XLA Modules:
  0.0 125.0 jit_solution(10724313648748129950)
XLA Ops:
  0.0 0.7 broadcast_compare_fusion
  0.7 0.1 gt.19
  0.8 0.0 copy-start.3
  0.8 0.0 copy-start.6
  0.8 0.0 copy-start.4
  0.8 0.0 copy-start.5
  0.8 0.0 copy-start.13
  0.9 7.2 %fusion.1.src = bf16[32,8,2048]{2,1,0:T(8,128)(2,1)} fusion(bf16[256,2048]{1,0:T(8,128)(2,1)} %constant.7.clone, bf16[2048,2048]{1,0:T(8,128)(2,1)} %bitcast.14, pred[2048]{0:T(1024)(128)(4,1)S(1)} %gt.19), kind=kOutput, calls=%fused_computation.3 | convolution fusion | flops 2148532224 | bytes 10487808 | tf_op jit(solution)/shard_map/dot_general | solution.py:298
  8.0 30.0 %shard_map.82.received = bf16[32,8,2048]{2,1,0:T(8,128)(2,1)} custom-call(bf16[32,8,2048]{2,1,0:T(8,128)(2,1)} %fusion.1.src), custom_call_target="tpu_custom_call" | custom-call | tf_op jit(solution)/shard_map/pallas_call | solution.py:140
  38.1 0.0 copy-done.3
  38.1 0.0 copy-done.6
  38.1 0.0 copy-start
  38.1 1.2 copy-done
  39.3 5.0 %shard_map.83 = (bf16[512,1024]{1,0:T(8,128)(2,1)S(1)}, f32[4,256,768]{2,1,0:T(8,128)}, f32[8,128]{1,0:T(8,128)S(1)}) custom-call(bf16[32,8,2048]{2,1,0:T(8,128)(2,1)S(1)} %copy-done, bf16[512,512]{1,0:T(8,128)(2,1)S(1)} %copy-done.6, bf16[512,768]{1,0:T(8,128)(2,1)S(1)} %copy-done.3), custom_call_target="tpu_custom_call" | custom-call | tf_op jit(solution)/shard_map/pallas_call | solution.py:308
  44.4 0.0 copy-start.7
  44.4 1.0 copy-done.7
  45.4 0.0 copy-start.12
  45.4 0.6 copy-done.12
  46.0 11.6 %shard_map.84.tops = f32[32,8,128]{2,1,0:T(8,128)} custom-call(f32[8,128]{1,0:T(8,128)} %copy-done.12), custom_call_target="tpu_custom_call" | custom-call | tf_op jit(solution)/shard_map/pallas_call | solution.py:156
  57.5 0.0 copy-done.4
  57.6 0.0 copy-done.5
  57.6 0.0 copy-done.13
  57.6 0.0 copy-start.8
  57.6 1.2 copy-done.8
  58.8 0.0 copy-start.9
  58.8 0.9 copy-done.9
  59.7 7.8 %shard_map.85 = (f32[4,256,768]{2,1,0:T(8,128)}, f32[8,128]{1,0:T(8,128)S(1)}) custom-call(s32[2]{0:T(128)S(1)} %copy-done.13, f32[32,8,128]{2,1,0:T(8,128)S(1)} %copy-done.9, f32[4,256,768]{2,1,0:T(8,128)} %get-tuple-element.11.old, bf16[512,1024]{1,0:T(8,128)(2,1)S(1)} %copy-done.8, bf16[768,512]{1,0:T(8,128)(2,1)S(1)} %copy-done.4, ...), custom_call_target="tpu_custom_call" | custom-call | tf_op jit(solution)/shard_map/pallas_call | solution.py:318
  67.5 0.0 copy-start.11
  67.5 0.6 copy-done.11
  68.1 10.7 %shard_map.86.tops = f32[32,8,128]{2,1,0:T(8,128)} custom-call(f32[8,128]{1,0:T(8,128)} %copy-done.11), custom_call_target="tpu_custom_call" | custom-call | tf_op jit(solution)/shard_map/pallas_call | solution.py:156
  78.8 0.0 copy-start.2
  78.8 1.9 %copy-done.2 = f32[4,256,768]{2,1,0:T(8,128)S(1)} copy-done((f32[4,256,768]{2,1,0:T(8,128)S(1)}, f32[4,256,768]{2,1,0:T(8,128)}, u32[]{:S(2)}) %copy-start.2) | copy-done | bytes 3145752
  80.7 0.0 copy-start.10
  80.7 0.9 copy-done.10
  81.6 0.0 copy-start.14
  81.6 4.0 %shard_map.87.src = bf16[32,8,2048]{2,1,0:T(8,128)(2,1)S(1)} custom-call(s32[2]{0:T(128)S(1)} %copy-done.13, f32[32,8,128]{2,1,0:T(8,128)S(1)} %copy-done.10, f32[4,256,768]{2,1,0:T(8,128)S(1)} %copy-done.2, bf16[768,512]{1,0:T(8,128)(2,1)S(1)} %copy-done.4, bf16[512,512]{1,0:T(8,128)(2,1)S(1)} %copy-done.5), custom_call_target="tpu_custom_call" | custom-call | tf_op jit(solution)/shard_map/pallas_call | solution.py:327
  85.6 0.0 copy-start.1
  85.7 1.0 copy-done.1
  86.6 30.0 %shard_map.88 = bf16[32,8,2048]{2,1,0:T(8,128)(2,1)} custom-call(bf16[32,8,2048]{2,1,0:T(8,128)(2,1)} %copy-done.1), custom_call_target="tpu_custom_call" | custom-call | tf_op jit(solution)/shard_map/pallas_call | solution.py:140
  116.6 1.5 %copy.9 = bf16[2048,256]{1,0:T(8,128)(2,1)S(1)} copy(bf16[2048,256]{0,1:T(8,128)(2,1)} %bitcast.12) | data formatting | bytes 2097152 | tf_op jit(solution)/shard_map/dot_general | solution.py:336
  118.1 0.0 copy-done.14
  118.1 6.9 %select_convert_fusion = bf16[32,64,2048]{2,1,0:T(8,128)(2,1)} fusion(bf16[32,64,2048]{2,1,0:T(8,128)(2,1)} %param.8, pred[32,64]{1,0:T(8,128)(4,1)S(1)} %broadcast_compare_fusion, bf16[32,64,256]{2,1,0:T(8,128)(2,1)S(1)} %bitcast.13, bf16[256,2048,1]{1,0,2:T(8,128)(2,1)S(1)} %copy-done.14), kind=kOutput, calls=%fused_computation | convolution fusion | flops 2164260864 | bytes 18876416 | tf_op jit(solution)/shard_map/dot_general | solution.py:336
Async XLA Ops:
  0.8 37.3 %copy-start.3 = (bf16[512,768]{1,0:T(8,128)(2,1)S(1)}, bf16[512,768]{1,0:T(8,128)(2,1)}, u32[]{:S(2)}) copy-start(bf16[512,768]{1,0:T(8,128)(2,1)} %constant.20.clone.tile) | copy-start | bytes 2359300
  0.8 37.3 %copy-start.6 = (bf16[512,512]{1,0:T(8,128)(2,1)S(1)}, bf16[512,512]{1,0:T(8,128)(2,1)}, u32[]{:S(2)}) copy-start(bf16[512,512]{1,0:T(8,128)(2,1)} %constant.18.clone.plane) | copy-start | bytes 1572868
  0.8 56.7 %copy-start.4 = (bf16[768,512]{1,0:T(8,128)(2,1)S(1)}, bf16[768,512]{1,0:T(8,128)(2,1)}, u32[]{:S(2)}) copy-start(bf16[768,512]{1,0:T(8,128)(2,1)} %constant.21.clone.inv_tile) | copy-start | bytes 2359300
  0.8 56.7 %copy-start.5 = (bf16[512,512]{1,0:T(8,128)(2,1)S(1)}, bf16[512,512]{1,0:T(8,128)(2,1)}, u32[]{:S(2)}) copy-start(bf16[512,512]{1,0:T(8,128)(2,1)} %constant.19.clone.inv_plane) | copy-start | bytes 1572868
  0.8 56.7 %copy-start.13 = (s32[2]{0:T(128)S(1)}, s32[2]{0:T(128)}, u32[]{:S(2)}) copy-start(s32[2]{0:T(128)} %levels.3) | copy-start | bytes 28
  38.1 1.2 copy-start
  44.4 1.0 copy-start.7
  45.4 0.6 copy-start.12
  57.6 1.2 copy-start.8
  58.8 0.9 copy-start.9
  67.5 0.6 copy-start.11
  78.8 1.9 %copy-start.2 = (f32[4,256,768]{2,1,0:T(8,128)S(1)}, f32[4,256,768]{2,1,0:T(8,128)}, u32[]{:S(2)}) copy-start(f32[4,256,768]{2,1,0:T(8,128)} %get-tuple-element.14.old) | copy-start | bytes 9437188
  80.7 0.9 copy-start.10
  81.6 36.5 %copy-start.14 = (bf16[256,2048,1]{1,0,2:T(8,128)(2,1)S(1)}, bf16[256,2048,1]{1,0,2:T(8,128)(2,1)}, u32[]{:S(2)}) copy-start(bf16[256,2048,1]{1,0,2:T(8,128)(2,1)} %constant.22) | copy-start | bytes 3145732
  85.6 1.0 copy-start.1

commit v2 on v1

v2 whole, which is shorter than its diff:
```python
import functools
import math

import jax
import jax.numpy as jnp
import numpy as np
from jax import lax
from jax.experimental import pallas as pl
from jax.experimental.pallas import tpu as pltpu
from jax.sharding import PartitionSpec as P

H = 16
NF = 128
FLO = 8
ITERS = 2
LANES = 128
MISSING = float(2.0**100)
FOUND = float(2.0**90)
MESH = pl.DeviceIdType.MESH
VM = pl.BlockSpec(memory_space=pltpu.VMEM)
SM = pl.BlockSpec(memory_space=pltpu.SMEM)
ANY = pl.BlockSpec(memory_space=pl.ANY)


def rounded(table):
    return np.asarray(table, np.float32).astype(jnp.bfloat16)


def angles(rows, columns, period):
    return (rows[:, None] * columns[None, :] % period) * (2.0 * math.pi / period)


def time_table(samples, devices):
    share = NF // devices
    phases = angles(FLO + np.arange(NF), np.arange(samples), samples)
    both = np.stack([np.cos(phases), -np.sin(phases)]).reshape(2, devices, share, samples)
    return rounded(both.transpose(1, 0, 2, 3).reshape(2 * NF, samples))


def plane_tables(positions):
    length = positions.shape[0]
    phases = angles(np.arange(length), positions, length)
    c, s = np.cos(phases), np.sin(phases)
    forward = np.block([[c, s], [-s, c]])
    c, s = c.T / length, s.T / length
    inverse = np.block([[c, -s], [s, c]])
    return rounded(forward), rounded(inverse)


def tile_tables(interior, extent):
    length = interior + 2 * H
    tiles = extent // interior
    offsets = np.arange(length)
    taper = np.where(
        offsets < 2 * H,
        np.sin(0.5 * math.pi * (offsets + 0.5) / (2 * H)),
        np.where(offsets >= interior, np.cos(0.5 * math.pi * (offsets - interior + 0.5) / (2 * H)), 1.0),
    )
    phases = angles(offsets, offsets, length)
    c, s = np.cos(phases), np.sin(phases)
    forward = np.zeros((2, extent, 2, tiles, length))
    inverse = np.zeros((2, tiles, length, 2, extent))
    ya, yb = taper[:, None] * c, taper[:, None] * s
    yc, yd = c * (taper / length)[None, :], s * (taper / length)[None, :]
    for j in range(tiles):
        at = (j * interior - H + offsets) % extent
        for o in range(length):
            forward[0, at[o], 0, j] += ya[o]
            forward[1, at[o], 0, j] += yb[o]
            forward[0, at[o], 1, j] -= yb[o]
            forward[1, at[o], 1, j] += ya[o]
            inverse[0, j, :, 0, at[o]] += yc[:, o]
            inverse[1, j, :, 0, at[o]] -= yd[:, o]
            inverse[0, j, :, 1, at[o]] += yd[:, o]
            inverse[1, j, :, 1, at[o]] += yc[:, o]
    wide = 2 * tiles * length
    return rounded(forward.reshape(2 * extent, wide)), rounded(inverse.reshape(wide, 2 * extent))


def greet_all(across, down, me):
    devices = across * down

    def greet(k, carry):
        peer = lax.rem(me + k, devices)
        pl.semaphore_signal(
            pltpu.get_barrier_semaphore(),
            inc=1,
            device_id=(peer // down, lax.rem(peer, down)),
            device_id_type=MESH,
        )
        return carry

    lax.fori_loop(1, devices, greet, 0)


def remote(down, peer, src, dst, send_sem, recv_sem):
    return pltpu.make_async_remote_copy(
        src_ref=src,
        dst_ref=dst,
        send_sem=send_sem,
        recv_sem=recv_sem,
        device_id=(peer // down, lax.rem(peer, down)),
        device_id_type=MESH,
    )


def dot(a, b):
    return jnp.dot(a, b, preferred_element_type=jnp.float32)


def analyse(sizes, grid, plane, tile, coeffs, peak):
    nx, ny, share, half = sizes
    best = jnp.zeros((8, LANES), jnp.float32)
    for f in range(share):
        turned = dot(plane[...], grid[:, f * ny : (f + 1) * ny]).astype(jnp.bfloat16)
        c = dot(jnp.concatenate([turned[:nx], turned[nx:]], axis=1), tile[...])
        coeffs[f] = c
        re, im = c[:, :half], c[:, half:]
        power = re * re + im * im
        best = jnp.maximum(best, jnp.max(power.reshape(-1, 8, half), axis=0)[:, :LANES])
        for part in range(1, half // LANES):
            best = jnp.maximum(
                best,
                jnp.max(power[:, part * LANES : (part + 1) * LANES].reshape(-1, 8, LANES), axis=0),
            )
    peak[...] = jnp.max(best, axis=0, keepdims=True)


def synthesise(sizes, level, tops, coeffs, plane, tile):
    nx, ny, share, half = sizes
    largest = jnp.sqrt(jnp.max(jnp.max(tops[...], axis=0), keepdims=True))
    cutoff = level.astype(jnp.float32) * 0.001 * (largest + 1e-06)
    for f in range(share):
        re, im = coeffs[f, :, :half], coeffs[f, :, half:]
        magnitude = jnp.sqrt(re * re + im * im)
        shrink = jnp.maximum(magnitude - cutoff, 0.0) / jnp.maximum(magnitude, cutoff)
        shrunk = jnp.concatenate(
            [(re * shrink).astype(jnp.bfloat16), (im * shrink).astype(jnp.bfloat16)], axis=1
        )
        lines = dot(shrunk, tile[...]).astype(jnp.bfloat16)
        yield f, dot(plane[...], jnp.concatenate([lines[:, :ny], lines[:, ny:]], axis=0))


def whole_kernel(
    sizes, shape, levels, spectra, plane, tile, inv_plane, inv_tile, returned,
    received, marked, grid, rebuilt, coeffs, peaks, tops, sent, left, right,
    out_send, out_recv, top_send, top_recv, back_send, back_recv, own_sem,
):
    across, down, interior, groups = shape
    nx, ny, share, half = sizes
    rows = 2 * share
    devices = across * down
    my_x, my_y = lax.axis_index("rx"), lax.axis_index("ry")
    me = my_x * down + my_y
    lower = lax.broadcasted_iota(jnp.int32, (groups, LANES), 1) < interior
    greet_all(across, down, me)
    pl.semaphore_wait(pltpu.get_barrier_semaphore(), devices - 1)

    def out_copy(peer, slot):
        return remote(down, peer, spectra.at[peer], received.at[slot], out_send.at[peer], out_recv.at[slot])

    def back_copy(peer, slot):
        return remote(down, peer, sent.at[peer], returned.at[slot], back_send.at[peer], back_recv.at[slot])

    def top_copy(iteration, peer, slot):
        return remote(
            down, peer, peaks.at[iteration], tops.at[iteration, slot],
            top_send.at[iteration, peer], top_recv.at[iteration, slot],
        )

    def send_out(k, carry):
        peer = lax.rem(my_x + k // down, across) * down + lax.rem(my_y + k % down, down)

        @pl.when(peer != me)
        def _():
            out_copy(peer, me).start()

        return carry

    lax.fori_loop(0, devices, send_out, 0)
    received[me] = spectra[me]

    def gather(k, carry):
        rx = lax.rem(my_x + across - k, across)
        for ry in range(down):
            peer = rx * down + ry

            @pl.when(peer != me)
            def _():
                out_copy(peer, peer).wait_recv()

        for pair in range(down // 2):
            for at, ref in ((0, left), (1, right)):
                block = received[rx * down + 2 * pair + at].astype(jnp.float32)
                for g in range(groups):
                    ref[g * rows : (g + 1) * rows] = block[:, g * LANES : (g + 1) * LANES]
            for r in range(rows):
                p, f = r // share, r % share
                a = left[pl.ds(r, groups, stride=rows)]
                b = right[pl.ds(r, groups, stride=rows)]
                first = jnp.where(lower, a, pltpu.roll(b, interior, 1)).astype(jnp.bfloat16)
                second = jnp.where(lower, pltpu.roll(a, interior, 1), b).astype(jnp.bfloat16)
                lanes = slice(f * ny + pair * LANES, f * ny + (pair + 1) * LANES)
                for xa, value in ((0, first), (1, second)):
                    row = pl.multiple_of(p * nx + (xa * across + rx) * groups, groups)
                    marked[pl.ds(row, groups), lanes] = value
        return carry

    lax.fori_loop(0, across, gather, 0)
    for iteration in range(ITERS):
        for f in range(share):
            lanes = slice(f * ny, (f + 1) * ny)
            seen = marked[:, lanes].astype(jnp.float32)
            other = rebuilt[:, lanes] if iteration else 0.0
            grid[:, lanes] = jnp.where(seen > FOUND, other, seen).astype(jnp.bfloat16)
        analyse(sizes, grid, plane, tile, coeffs, peaks.at[iteration])

        def send_top(k, carry):
            top_copy(iteration, lax.rem(me + k, devices), me).start()
            return carry

        def wait_top(k, carry):
            peer = lax.rem(me + k, devices)
            top_copy(iteration, peer, peer).wait()
            return carry

        lax.fori_loop(1, devices, send_top, 0)
        tops[iteration, me] = peaks[iteration]
        lax.fori_loop(1, devices, wait_top, 0)
        for f, back in synthesise(sizes, levels[iteration], tops.at[iteration], coeffs, inv_plane, inv_tile):
            rebuilt[:, f * ny : (f + 1) * ny] = back

    def spread(k, carry):
        rx = lax.rem(my_x + k, across)
        for pair in range(down // 2):
            for r in range(rows):
                p, f = r // share, r % share
                lanes = slice(f * ny + pair * LANES, f * ny + (pair + 1) * LANES)
                first, second = (
                    rebuilt[pl.ds(pl.multiple_of(p * nx + (xa * across + rx) * groups, groups), groups), lanes]
                    for xa in range(2)
                )
                left[pl.ds(r, groups, stride=rows)] = jnp.where(lower, first, pltpu.roll(second, interior, 1))
                right[pl.ds(r, groups, stride=rows)] = jnp.where(lower, pltpu.roll(first, interior, 1), second)
            for at, ref in ((0, left), (1, right)):
                for g in range(groups):
                    sent[rx * down + 2 * pair + at, :, g * LANES : (g + 1) * LANES] = ref[
                        g * rows : (g + 1) * rows
                    ].astype(jnp.bfloat16)
        for ry in range(down):
            peer = rx * down + ry

            @pl.when(peer != me)
            def _():
                back_copy(peer, me).start()

        return carry

    lax.fori_loop(0, across, spread, 0)
    own = pltpu.make_async_copy(sent.at[me], returned.at[me], own_sem)
    own.start()
    own.wait()

    def finish(k, carry):
        peer = lax.rem(me + k, devices)
        out_copy(peer, peer).wait_send()
        back_copy(peer, peer).wait()
        return carry

    lax.fori_loop(1, devices, finish, 0)


def body(across, down, record, sampled, levels):
    rows_x, rows_y, samples = record.shape
    devices = across * down
    share = NF // devices
    rows = 2 * share
    nx, ny = rows_x * across, rows_y * down
    traces = rows_x * rows_y
    pack = LANES // rows_y
    groups = traces // LANES
    assert pack == 2 and down % 2 == 0
    half = ny // rows_y * (rows_y + 2 * H)
    sizes = (nx, ny, share, half)
    shape = (across, down, rows_y, groups)
    times = jnp.asarray(time_table(samples, devices))
    ids = np.arange(nx)
    xa, rx, g = ids // (across * groups), ids // groups % across, ids % groups
    plane, inv_plane = map(jnp.asarray, plane_tables(rx * rows_x + g * pack + xa))
    tile, inv_tile = map(jnp.asarray, tile_tables(rows_y, ny))
    flat = record.reshape(traces, samples)
    spectra = lax.dot_general(
        times, flat, (((1,), (1,)), ((), ())), preferred_element_type=jnp.float32
    )
    spectra = jnp.where(sampled.reshape(1, traces) > 0, spectra, MISSING).astype(jnp.bfloat16)
    block_shape = (devices, rows, traces)
    grid_shape = (2 * nx, share * ny)
    sem = pltpu.SemaphoreType.DMA
    returned = pl.pallas_call(
        functools.partial(whole_kernel, sizes, shape),
        out_shape=jax.ShapeDtypeStruct(block_shape, jnp.bfloat16),
        in_specs=[SM] + [VM] * 5,
        out_specs=VM,
        scratch_shapes=[
            pltpu.VMEM(block_shape, jnp.bfloat16),
            pltpu.VMEM(grid_shape, jnp.bfloat16),
            pltpu.VMEM(grid_shape, jnp.bfloat16),
            pltpu.VMEM(grid_shape, jnp.float32),
            pltpu.VMEM((share, nx, 2 * half), jnp.float32),
            pltpu.VMEM((ITERS, 1, LANES), jnp.float32),
            pltpu.VMEM((ITERS, devices, 1, LANES), jnp.float32),
            pltpu.VMEM(block_shape, jnp.bfloat16),
            pltpu.VMEM((groups * rows, LANES), jnp.float32),
            pltpu.VMEM((groups * rows, LANES), jnp.float32),
            sem((devices,)),
            sem((devices,)),
            sem((ITERS, devices)),
            sem((ITERS, devices)),
            sem((devices,)),
            sem((devices,)),
            sem,
        ],
        compiler_params=pltpu.CompilerParams(
            collective_id=0, has_side_effects=True, vmem_limit_bytes=48 * 1024 * 1024
        ),
    )(levels, spectra.reshape(block_shape), plane, tile, inv_plane, inv_tile)
    recon = lax.dot_general(
        returned.reshape(2 * NF, traces), times, (((0,), (0,)), ((), ())),
        preferred_element_type=jnp.float32,
    ).reshape(rows_x, rows_y, samples) * (2.0 / samples)
    return jnp.where(sampled[:, :, None] > 0, record.astype(jnp.float32), recon).astype(jnp.bfloat16)


def solution(mesh):
    return jax.shard_map(
        functools.partial(body, mesh.shape["rx"], mesh.shape["ry"]),
        mesh=mesh,
        in_specs=(P("rx", "ry", None), P("rx", "ry"), P()),
        out_specs=P("rx", "ry", None),
        check_vma=False,
    )
```

time: 127 us -> 90.8 us (0.71); the launches traced: 125 us -> 90.6 us
  Pallas kernels: 99.2 us -> 75.7 us
  local copies, waits for them, and re-layouts: 10.8 us -> 0.63 us
    pallas_call x7 -> x1, Pallas kernels: 99.2 us -> 75.7 us  [body(): pl.pallas_call(functools.partial(whole_kernel, sizes, shape), out_shape=j...]
    unnamed x30 -> x10, local copies, waits for them, and re-layouts: 9.28 us -> 0.02 us
where the time goes in v2:
time: 90.8 us; the launch traced here: 90.6 us
  Pallas kernels  75.7 us (83%)
  matrix products  13.3 us (15%)
    pallas_call x1, Pallas kernels, body(): pl.pallas_call(functools.partial(whole_kernel, sizes, shape), out_shape=j...  75.7 us
    dot_general x1, matrix products, body(): lax.dot_general(returned.reshape(2 * NF, traces), times, (((0,), (0,)), (...  7.18 us
    dot_general x1, matrix products, body(): lax.dot_general(times, flat, (((1,), (1,)), ((), ())), preferred_element_...  6.13 us

profile of v2, /device:TPU:9, one launch (start us, length us, event | category | flops | bytes accessed | tf_op | source)
XLA Modules:
  0.0 90.6 jit_solution(10524742716748167656)
XLA Ops:
  0.0 0.0 copy-start
  0.0 0.0 copy-start.1
  0.0 0.0 copy-start.2
  0.0 0.0 copy-start.4
  0.0 0.9 broadcast_compare_fusion
  0.9 0.1 gt.19
  1.0 0.0 copy-start.3
  1.0 6.1 %fusion.1.spectra = bf16[32,8,2048]{2,1,0:T(8,128)(2,1)S(1)} fusion(bf16[256,2048]{1,0:T(8,128)(2,1)} %constant.7.clone, bf16[2048,2048]{1,0:T(8,128)(2,1)} %bitcast.14, pred[2048]{0:T(1024)(128)(4,1)S(1)} %gt.19), kind=kOutput, calls=%fused_computation.3 | convolution fusion | flops 2148532224 | bytes 10487808 | tf_op jit(solution)/shard_map/dot_general | solution.py:292
  7.1 0.0 copy-done
  7.1 0.0 copy-done.1
  7.1 0.0 copy-done.2
  7.1 0.0 copy-done.4
  7.2 0.0 copy-done.3
  7.2 75.7 %shard_map.82 = bf16[32,8,2048]{2,1,0:T(8,128)(2,1)S(1)} custom-call(s32[2]{0:T(128)S(1)} %copy-done.4, bf16[32,8,2048]{2,1,0:T(8,128)(2,1)S(1)} %fusion.1.spectra, bf16[512,512]{1,0:T(8,128)(2,1)S(1)} %copy-done.3, bf16[512,768]{1,0:T(8,128)(2,1)S(1)} %copy-done.1, bf16[512,512]{1,0:T(8,128)(2,1)S(1)} %copy-done.2, bf16[768,512]{1,0:T(8,128)(2,1)S(1)} %copy-done), custom_call_target="tpu_custom_call" | custom-call | tf_op jit(solution)/shard_map/pallas_call | solution.py:299
  82.9 0.5 copy.9
  83.4 7.2 %select_convert_fusion = bf16[32,64,2048]{2,1,0:T(8,128)(2,1)} fusion(bf16[32,64,2048]{2,1,0:T(8,128)(2,1)} %param.8, pred[32,64]{1,0:T(8,128)(4,1)S(1)} %broadcast_compare_fusion, bf16[32,64,256]{2,1,0:T(8,128)(2,1)S(1)} %bitcast.13, bf16[256,2048,1]{1,0,2:T(8,128)(2,1)} %constant.22), kind=kOutput, calls=%fused_computation | convolution fusion | flops 2164260864 | bytes 18876416 | tf_op jit(solution)/shard_map/dot_general | solution.py:327
Async XLA Ops:
  0.0 7.1 %copy-start = (bf16[768,512]{1,0:T(8,128)(2,1)S(1)}, bf16[768,512]{1,0:T(8,128)(2,1)}, u32[]{:S(2)}) copy-start(bf16[768,512]{1,0:T(8,128)(2,1)} %constant.21.clone.inv_tile) | copy-start | bytes 2359300
  0.0 7.1 %copy-start.1 = (bf16[512,768]{1,0:T(8,128)(2,1)S(1)}, bf16[512,768]{1,0:T(8,128)(2,1)}, u32[]{:S(2)}) copy-start(bf16[512,768]{1,0:T(8,128)(2,1)} %constant.20.clone.tile) | copy-start | bytes 2359300
  0.0 7.1 %copy-start.2 = (bf16[512,512]{1,0:T(8,128)(2,1)S(1)}, bf16[512,512]{1,0:T(8,128)(2,1)}, u32[]{:S(2)}) copy-start(bf16[512,512]{1,0:T(8,128)(2,1)} %constant.19.clone.inv_plane) | copy-start | bytes 1572868
  0.0 7.1 %copy-start.4 = (s32[2]{0:T(128)S(1)}, s32[2]{0:T(128)}, u32[]{:S(2)}) copy-start(s32[2]{0:T(128)} %levels.1) | copy-start | bytes 28
  1.0 6.2 %copy-start.3 = (bf16[512,512]{1,0:T(8,128)(2,1)S(1)}, bf16[512,512]{1,0:T(8,128)(2,1)}, u32[]{:S(2)}) copy-start(bf16[512,512]{1,0:T(8,128)(2,1)} %constant.18.clone.plane) | copy-start | bytes 1572868

commit v3 on v2

--- a/solution.py
+++ b/solution.py
@@ -14,6 +14,8 @@
 FLO = 8
 ITERS = 2
 LANES = 128
+LOADS = 4
+SENDS = 2
 MISSING = float(2.0**100)
 FOUND = float(2.0**90)
 MESH = pl.DeviceIdType.MESH
@@ -142,9 +144,9 @@
 
 
 def whole_kernel(
-    sizes, shape, levels, spectra, plane, tile, inv_plane, inv_tile, returned,
-    received, marked, grid, rebuilt, coeffs, peaks, tops, sent, left, right,
-    out_send, out_recv, top_send, top_recv, back_send, back_recv, own_sem,
+    sizes, shape, levels, record, kept, times, plane, tile, inv_plane, inv_tile, returned,
+    samples, spectra, received, marked, grid, rebuilt, coeffs, peaks, tops, sent, left, right,
+    out_send, out_recv, top_send, top_recv, back_send, back_recv, own_sem, load_sem,
 ):
     across, down, interior, groups = shape
     nx, ny, share, half = sizes
@@ -153,11 +155,24 @@
     my_x, my_y = lax.axis_index("rx"), lax.axis_index("ry")
     me = my_x * down + my_y
     lower = lax.broadcasted_iota(jnp.int32, (groups, LANES), 1) < interior
+    traces = groups * LANES
+    loads, piece = samples.shape[:2]
+    per_send = loads // SENDS
+    part = traces // SENDS
+
+    def load(c):
+        return pltpu.make_async_copy(record.at[pl.ds(c * piece, piece)], samples.at[c], load_sem.at[c])
+
+    for c in range(loads):
+        load(c).start()
     greet_all(across, down, me)
-    pl.semaphore_wait(pltpu.get_barrier_semaphore(), devices - 1)
-
-    def out_copy(peer, slot):
-        return remote(down, peer, spectra.at[peer], received.at[slot], out_send.at[peer], out_recv.at[slot])
+
+    def out_copy(h, peer, slot):
+        lanes = pl.ds(h * part, part)
+        return remote(
+            down, peer, spectra.at[peer, :, lanes], received.at[slot, :, lanes],
+            out_send.at[h, peer], out_recv.at[h, slot],
+        )
 
     def back_copy(peer, slot):
         return remote(down, peer, sent.at[peer], returned.at[slot], back_send.at[peer], back_recv.at[slot])
@@ -168,16 +183,29 @@
             top_send.at[iteration, peer], top_recv.at[iteration, slot],
         )
 
-    def send_out(k, carry):
-        peer = lax.rem(my_x + k // down, across) * down + lax.rem(my_y + k % down, down)
-
-        @pl.when(peer != me)
-        def _():
-            out_copy(peer, me).start()
-
-        return carry
-
-    lax.fori_loop(0, devices, send_out, 0)
+    for h in range(SENDS):
+        for c in range(h * per_send, (h + 1) * per_send):
+            lanes = slice(c * piece, (c + 1) * piece)
+            load(c).wait()
+            lines = lax.dot_general(
+                times[...], samples[c], (((1,), (1,)), ((), ())), preferred_element_type=jnp.float32
+            )
+            lines = jnp.where(kept[:, lanes] > 0, lines, MISSING)
+            for d in range(devices):
+                spectra[d, :, lanes] = lines[d * rows : (d + 1) * rows].astype(jnp.bfloat16)
+        if h == 0:
+            pl.semaphore_wait(pltpu.get_barrier_semaphore(), devices - 1)
+
+        def send_out(k, carry):
+            peer = lax.rem(my_x + k // down, across) * down + lax.rem(my_y + k % down, down)
+
+            @pl.when(peer != me)
+            def _():
+                out_copy(h, peer, me).start()
+
+            return carry
+
+        lax.fori_loop(0, devices, send_out, 0)
     received[me] = spectra[me]
 
     def gather(k, carry):
@@ -187,7 +215,8 @@
 
             @pl.when(peer != me)
             def _():
-                out_copy(peer, peer).wait_recv()
+                for h in range(SENDS):
+                    out_copy(h, peer, peer).wait_recv()
 
         for pair in range(down // 2):
             for at, ref in ((0, left), (1, right)):
@@ -263,7 +292,8 @@
 
     def finish(k, carry):
         peer = lax.rem(me + k, devices)
-        out_copy(peer, peer).wait_send()
+        for h in range(SENDS):
+            out_copy(h, peer, peer).wait_send()
         back_copy(peer, peer).wait()
         return carry
 
@@ -289,19 +319,17 @@
     plane, inv_plane = map(jnp.asarray, plane_tables(rx * rows_x + g * pack + xa))
     tile, inv_tile = map(jnp.asarray, tile_tables(rows_y, ny))
     flat = record.reshape(traces, samples)
-    spectra = lax.dot_general(
-        times, flat, (((1,), (1,)), ((), ())), preferred_element_type=jnp.float32
-    )
-    spectra = jnp.where(sampled.reshape(1, traces) > 0, spectra, MISSING).astype(jnp.bfloat16)
     block_shape = (devices, rows, traces)
     grid_shape = (2 * nx, share * ny)
     sem = pltpu.SemaphoreType.DMA
     returned = pl.pallas_call(
         functools.partial(whole_kernel, sizes, shape),
         out_shape=jax.ShapeDtypeStruct(block_shape, jnp.bfloat16),
-        in_specs=[SM] + [VM] * 5,
+        in_specs=[SM, ANY] + [VM] * 6,
         out_specs=VM,
         scratch_shapes=[
+            pltpu.VMEM((LOADS, traces // LOADS, samples), jnp.bfloat16),
+            pltpu.VMEM(block_shape, jnp.bfloat16),
             pltpu.VMEM(block_shape, jnp.bfloat16),
             pltpu.VMEM(grid_shape, jnp.bfloat16),
             pltpu.VMEM(grid_shape, jnp.bfloat16),
@@ -312,18 +340,19 @@
             pltpu.VMEM(block_shape, jnp.bfloat16),
             pltpu.VMEM((groups * rows, LANES), jnp.float32),
             pltpu.VMEM((groups * rows, LANES), jnp.float32),
-            sem((devices,)),
-            sem((devices,)),
+            sem((SENDS, devices)),
+            sem((SENDS, devices)),
             sem((ITERS, devices)),
             sem((ITERS, devices)),
             sem((devices,)),
             sem((devices,)),
             sem,
+            sem((LOADS,)),
         ],
         compiler_params=pltpu.CompilerParams(
             collective_id=0, has_side_effects=True, vmem_limit_bytes=48 * 1024 * 1024
         ),
-    )(levels, spectra.reshape(block_shape), plane, tile, inv_plane, inv_tile)
+    )(levels, flat, sampled.reshape(1, traces), times, plane, tile, inv_plane, inv_tile)
     recon = lax.dot_general(
         returned.reshape(2 * NF, traces), times, (((0,), (0,)), ((), ())),
         preferred_element_type=jnp.float32,

time: 90.8 us -> 91.9 us (1.012)
  local copies, waits for them, and re-layouts: 0.63 us -> 7.55 us
  matrix products: 13.3 us -> 6.9 us
    unnamed x10 -> x14, local copies, waits for them, and re-layouts: 0.02 us -> 6.23 us
    dot_general x1 -> x0, matrix products: 6.13 us -> none  [body(): lax.dot_general(times, flat, (((1,), (1,)), ((), ())), preferred_element_...]
where the time goes in v3:
time: 91.9 us; the launch traced here: 91.4 us
  Pallas kernels  76.2 us (83%)
  local copies, waits for them, and re-layouts  7.55 us (8%)
  matrix products  6.9 us (8%)
    pallas_call x1, Pallas kernels, body(): pl.pallas_call(functools.partial(whole_kernel, sizes, shape), out_shape=j...  76.2 us
    dot_general x1, matrix products, body(): lax.dot_general(returned.reshape(2 * NF, traces), times, (((0,), (0,)), (...  6.9 us
    unnamed x14, local copies, waits for them, and re-layouts  6.23 us

profile of v3, /device:TPU:9, one launch (start us, length us, event | category | flops | bytes accessed | tf_op | source)
XLA Modules:
  0.0 91.4 jit_solution(15406067550054879002)
XLA Ops:
  0.0 0.7 broadcast_compare_fusion
  0.7 0.8 reshape.14.kept
  1.5 0.0 copy-start
  1.5 1.2 %copy-done = bf16[256,2048]{1,0:T(8,128)(2,1)S(1)} copy-done((bf16[256,2048]{1,0:T(8,128)(2,1)S(1)}, bf16[256,2048]{1,0:T(8,128)(2,1)}, u32[]{:S(2)}) %copy-start) | copy-done | bytes 1048600
  2.7 0.0 copy-start.1
  2.7 1.1 %copy-done.1 = bf16[768,512]{1,0:T(8,128)(2,1)S(1)} copy-done((bf16[768,512]{1,0:T(8,128)(2,1)S(1)}, bf16[768,512]{1,0:T(8,128)(2,1)}, u32[]{:S(2)}) %copy-start.1) | copy-done | bytes 786456
  3.9 0.0 copy-start.2
  3.9 1.1 %copy-done.2 = bf16[512,768]{1,0:T(8,128)(2,1)S(1)} copy-done((bf16[512,768]{1,0:T(8,128)(2,1)S(1)}, bf16[512,768]{1,0:T(8,128)(2,1)}, u32[]{:S(2)}) %copy-start.2) | copy-done | bytes 786456
  5.0 0.0 copy-start.3
  5.0 1.0 %copy-done.3 = bf16[512,512]{1,0:T(8,128)(2,1)S(1)} copy-done((bf16[512,512]{1,0:T(8,128)(2,1)S(1)}, bf16[512,512]{1,0:T(8,128)(2,1)}, u32[]{:S(2)}) %copy-start.3) | copy-done | bytes 524312
  6.1 0.0 copy-start.4
  6.1 1.0 %copy-done.4 = bf16[512,512]{1,0:T(8,128)(2,1)S(1)} copy-done((bf16[512,512]{1,0:T(8,128)(2,1)S(1)}, bf16[512,512]{1,0:T(8,128)(2,1)}, u32[]{:S(2)}) %copy-start.4) | copy-done | bytes 524312
  7.1 0.0 copy-start.5
  7.1 0.7 copy-done.5
  7.8 0.0 copy-start.6
  7.8 76.2 %shard_map.82 = bf16[32,8,2048]{2,1,0:T(8,128)(2,1)S(1)} custom-call(s32[2]{0:T(128)S(1)} %copy-done.5, bf16[2048,2048]{1,0:T(8,128)(2,1)} %bitcast.9, s32[1,2048]{1,0:T(1,128)S(1)} %reshape.14.kept, bf16[256,2048]{1,0:T(8,128)(2,1)S(1)} %copy-done, bf16[512,512]{1,0:T(8,128)(2,1)S(1)} %copy-done.4, bf16[512,768]{1,0:T(8,128)(2,1)S(1)} %copy-done.2, ...), custom_call_target="tpu_custom_call" | custom-call | tf_op jit(solution)/shard_map/pallas_call | solution.py:325
  84.0 0.5 copy.9
  84.5 0.0 copy-done.6
  84.5 6.9 %select_convert_fusion = bf16[32,64,2048]{2,1,0:T(8,128)(2,1)} fusion(bf16[32,64,2048]{2,1,0:T(8,128)(2,1)} %param.8, pred[32,64]{1,0:T(8,128)(4,1)S(1)} %broadcast_compare_fusion, bf16[32,64,256]{2,1,0:T(8,128)(2,1)S(1)} %bitcast.10, bf16[256,2048,1]{1,0,2:T(8,128)(2,1)S(1)} %copy-done.6), kind=kOutput, calls=%fused_computation | convolution fusion | flops 2164260864 | bytes 18876416 | tf_op jit(solution)/shard_map/dot_general | solution.py:356
Async XLA Ops:
  1.5 1.2 %copy-start = (bf16[256,2048]{1,0:T(8,128)(2,1)S(1)}, bf16[256,2048]{1,0:T(8,128)(2,1)}, u32[]{:S(2)}) copy-start(bf16[256,2048]{1,0:T(8,128)(2,1)} %constant.14.clone.times) | copy-start | bytes 3145732
  2.7 1.1 %copy-start.1 = (bf16[768,512]{1,0:T(8,128)(2,1)S(1)}, bf16[768,512]{1,0:T(8,128)(2,1)}, u32[]{:S(2)}) copy-start(bf16[768,512]{1,0:T(8,128)(2,1)} %constant.18.clone.inv_tile) | copy-start | bytes 2359300
  3.9 1.1 %copy-start.2 = (bf16[512,768]{1,0:T(8,128)(2,1)S(1)}, bf16[512,768]{1,0:T(8,128)(2,1)}, u32[]{:S(2)}) copy-start(bf16[512,768]{1,0:T(8,128)(2,1)} %constant.17.clone.tile) | copy-start | bytes 2359300
  5.0 1.0 %copy-start.3 = (bf16[512,512]{1,0:T(8,128)(2,1)S(1)}, bf16[512,512]{1,0:T(8,128)(2,1)}, u32[]{:S(2)}) copy-start(bf16[512,512]{1,0:T(8,128)(2,1)} %constant.16.clone.inv_plane) | copy-start | bytes 1572868
  6.1 1.0 %copy-start.4 = (bf16[512,512]{1,0:T(8,128)(2,1)S(1)}, bf16[512,512]{1,0:T(8,128)(2,1)}, u32[]{:S(2)}) copy-start(bf16[512,512]{1,0:T(8,128)(2,1)} %constant.15.clone.plane) | copy-start | bytes 1572868
  7.1 0.7 copy-start.5
  7.8 76.8 %copy-start.6 = (bf16[256,2048,1]{1,0,2:T(8,128)(2,1)S(1)}, bf16[256,2048,1]{1,0,2:T(8,128)(2,1)}, u32[]{:S(2)}) copy-start(bf16[256,2048,1]{1,0,2:T(8,128)(2,1)} %constant.19) | copy-start | bytes 3145732
